TPU v7x, 256 devices: a whole 4x4x8 slice. The times are simulated.
256 devices in a mesh: rows: 8 (over x, core), pts: 32 (over y, z).
Axes of the slice: x: 4, y: 4, z: 8, core: 2. Of those that a mesh axis runs over, the one named last changes fastest.
Arguments:
- features: bfloat16 [32768, 128], P('pts'), may hold values from -6 to 6
- targets: bfloat16 [32768, 256], P('pts'), may hold values from -6 to 6
- coefficients: float32 [32768, 256], P('pts'), may hold values from -6 to 6
- momentum: float32 [32768, 256], P('pts'), may hold values from -6 to 6
- block_index: int32 [2, 2048], replicated, may hold values from 0 to 32767, as said below
- pivot_index: int32 [2, 512], replicated, may hold values from 0 to 2047, as said below
- nystrom_core: bfloat16 [2, 512, 512], replicated, may hold values from -0.5 to 3
Outputs:
- new_coefficients: float32 [32768, 256], P('pts')
- new_momentum: float32 [32768, 256], P('pts')
Inputs may be any that keep to these rules, and one draw needn't show every extreme that they name: `block_index`: each row lists 2048 distinct points; a point p belongs to index p // 1024 of pts; in each row one index of pts, drawn from the seed, owns exactly 24 of the points in every aligned group of 256 positions, and no index owns more than 24 points of any such group. `pivot_index`: each row lists 512 distinct positions.
All inputs are finite; a program needn't handle non-finite values.
Results may differ from a plain program's by a relative error of at most 0.0041.
The roundings to bfloat16 on the way count: a program that leaves them out, or rounds other values in their place, can miss the bound.
Values may be sent and summed in bfloat16 or wider, within the bound.
A program may use at most 64 MiB of HBM per device.

v0:
```python
import jax
import jax.numpy as jnp
from jax import lax
from jax.sharding import PartitionSpec as P

UPDATES = 2
alpha_mix = 0.6
beta_keep = 0.9
step_size = 0.2
momentum_gain = 1.5
ridge_term = 1.0


def kernel_tile(left_rows, right_rows):
    inner_prod = lax.dot_general(
        left_rows, right_rows, (((1,), (1,)), ((), ())), preferred_element_type=jnp.float32
    )
    left_sq = jnp.sum(jnp.square(left_rows.astype(jnp.float32)), axis=1)
    right_sq = jnp.sum(jnp.square(right_rows.astype(jnp.float32)), axis=1)
    squared = left_sq[:, None] + right_sq[None, :] - 2.0 * inner_prod
    return jnp.exp(squared * (-3.5 / left_rows.shape[1])).astype(jnp.bfloat16)


def project_rows(factor, resid):
    return lax.dot_general(
        factor,
        resid.astype(jnp.bfloat16),
        (((0,), (0,)), ((), ())),
        preferred_element_type=jnp.float32,
    )


def finish_step(resid, factor, proj, core_now):
    lifted = jnp.dot(
        core_now, proj.astype(jnp.bfloat16), preferred_element_type=jnp.float32
    ).astype(jnp.bfloat16)
    return (resid - jnp.dot(factor, lifted, preferred_element_type=jnp.float32)).astype(
        jnp.bfloat16
    )


def owned_rows(local_feats, wanted, first_point):
    local_pos = wanted - first_point
    holder = (local_pos >= 0) & (local_pos < local_feats.shape[0])
    safe_pos = jnp.clip(local_pos, 0, local_feats.shape[0] - 1)
    return (holder, safe_pos)


def shards(features, targets, coefficients, momentum, block_index, pivot_index, nystrom_core):
    row_count = lax.axis_size("rows")
    pts_count = lax.axis_size("pts")
    row_id = lax.axis_index("rows")
    pts_id = lax.axis_index("pts")
    local_points = features.shape[0]
    per_row = block_index.shape[1] // row_count
    per_device = per_row // pts_count
    first_point = pts_id * local_points
    current = coefficients
    momentum_now = momentum
    for update in range(UPDATES):
        mixed = alpha_mix * momentum_now + (1.0 - alpha_mix) * current
        mixed_bf = mixed.astype(jnp.bfloat16)
        whole_index = block_index[update]
        row_points = lax.dynamic_slice_in_dim(whole_index, row_id * per_row, per_row)
        holder, safe_pos = owned_rows(features, row_points, first_point)
        row_terms = jnp.where(holder[:, None], features[safe_pos], jnp.zeros((), jnp.bfloat16))
        offset = jnp.where(
            holder[:, None],
            ridge_term * mixed[safe_pos] - targets[safe_pos].astype(jnp.float32),
            0.0,
        )
        pivot_points = whole_index[pivot_index[update]]
        pivot_holder, pivot_pos = owned_rows(features, pivot_points, first_point)
        pivot_terms = jnp.where(
            pivot_holder[:, None], features[pivot_pos], jnp.zeros((), jnp.bfloat16)
        )
        got_rows, got_pivots = (
            lax.psum(row_terms, "pts").astype(jnp.float32),
            lax.psum(pivot_terms, "pts").astype(jnp.float32),
        )
        block_feats = got_rows.astype(jnp.bfloat16)
        pivot_feats = got_pivots.astype(jnp.bfloat16)
        partial_value = (
            jnp.dot(
                kernel_tile(block_feats, features), mixed_bf, preferred_element_type=jnp.float32
            )
            + offset
        )
        local_all = whole_index - first_point
        whole_slots = jnp.where(
            (local_all >= 0) & (local_all < local_points), local_all, local_points
        )
        resid = lax.psum_scatter(partial_value, "pts", scatter_dimension=0, tiled=True)
        share_feats = lax.dynamic_slice_in_dim(block_feats, pts_id * per_device, per_device)
        factor = kernel_tile(share_feats, pivot_feats)
        proj = lax.psum(project_rows(factor, resid), ("rows", "pts"))
        step_bf = finish_step(resid, factor, proj, nystrom_core[update])
        steps = lax.all_gather(step_bf, ("rows", "pts"), axis=0, tiled=True)
        change = steps.astype(jnp.float32)
        current = mixed.at[whole_slots].add(-step_size * change, mode="drop")
        momentum_now = (
            (beta_keep * momentum_now + (1.0 - beta_keep) * mixed)
            .at[whole_slots]
            .add(-step_size * momentum_gain * change, mode="drop")
        )
    return (current, momentum_now)


def solution(mesh):
    in_specs = (P("pts", None), P("pts", None), P("pts", None), P("pts", None), P(), P(), P())
    out_specs = (P("pts", None), P("pts", None))
    return jax.shard_map(shards, mesh=mesh, in_specs=in_specs, out_specs=out_specs, check_vma=False)
```

profile of v0, /device:TPU:1, one launch (start us, length us, event | category | flops | bytes accessed | tf_op | source)
XLA Modules:
  0.0 1027.0 jit_solution(4563416117021022142)
XLA Ops:
  7.2 0.8 fusion.70
  8.9 3.1 gather_fusion.8
  12.1 3.1 gather_fusion.3
  15.3 0.9 gather_fusion
  16.2 1.3 gather_fusion.4
  17.5 0.9 gather_fusion.5
  18.4 1.3 gather_fusion.9
  22.9 2.6 multiply_add_fusion.2
  25.4 1.0 gather_fusion.1
  26.4 1.2 gather_fusion.2
  27.8 140.3 %all-reduce.5.cloned.1.call-done = (bf16[256,128]{1,0:T(8,128)(2,1)}, bf16[512,128]{1,0:T(8,128)(2,1)}, bf16[256,128]{1,0:T(8,128)(2,1)}, bf16[512,128]{1,0:T(8,128)(2,1)}) async-done(((bf16[256,128]{1,0:T(8,128)(2,1)}, bf16[512,128]{1,0:T(8,128)(2,1)}, bf16[256,128]{1,0:T(8,128)(2,1)}, bf16[512,128]{1,0:T(8,128)(2,1)}), (bf16[256,128]{1,0:T(8,128)(2,1)}, bf16[512,128]{1,0:T(8,128)(2,1)}, ...) | async-done | bytes 393232 | tf_op jit(solution)/shard_map/psum | solution.py:78
  168.1 0.9 multiply_reduce_fusion.4
  169.0 2.1 fusion.16
  172.2 0.8 fusion.24
  173.0 210.5 %reduce-scatter.3.cloned.1.call-done = f32[8,256]{1,0:T(8,128)} async-done(((f32[256,256]{1,0:T(8,128)}), f32[8,256]{1,0:T(8,128)}) %reduce-scatter.3.cloned.1.call-update) | async-done | bytes 8208 | tf_op jit(solution)/shard_map/reduce_scatter | solution.py:93
  383.5 1.0 fusion.60
  384.6 83.0 %all-reduce.6 = bf16[512,256]{1,0:T(8,128)(2,1)S(1)} all-reduce(f32[512,256]{1,0:T(8,128)S(1)} %fusion.60), channel_id=1, replica_groups=mesh['rows'=8,'pts'=32] {'rows','pts'}, use_global_device_ids=true, to_apply=%region_7.8 | all-reduce | flops 131072 | bytes 786432 | tf_op jit(solution)/shard_map/psum | solution.py:96
  467.6 2.1 fusion.28
  469.8 1.2 gather_fusion.7
  471.1 98.4 %all-gather.3.cloned.1.call-done = bf16[2048,256]{1,0:T(8,128)(2,1)} async-done(((bf16[8,256]{1,0:T(8,128)(2,1)}), bf16[2048,256]{1,0:T(8,128)(2,1)}) %all-gather.3.cloned.1.call-update) | async-done | bytes 1048592 | tf_op jit(solution)/shard_map/all_gather | solution.py:98
  569.5 12.7 %scatter_custom_fusion.1 = f32[1024,256]{1,0:T(8,128)S(1)} fusion(f32[1024,256]{1,0:T(8,128)S(1)} %get-tuple-element.9, s32[2048]{0:T(1024)S(1)} %bitcast.54, bf16[2048,256]{1,0:T(8,128)(2,1)} %all-gather.3.cloned.1.call-done, f32[]{:T(128)} %constant.14.clone.1), kind=kCustom, calls=%fused_computation.19 | custom fusion | flops 1572864 | bytes 2097156 | tf_op jit(solution)/shard_map/scatter-add | solution.py:100
  582.2 13.8 %scatter_custom_fusion = f32[1024,256]{1,0:T(8,128)} fusion(f32[1024,256]{1,0:T(8,128)} %get-tuple-element.8, s32[2048]{0:T(1024)S(1)} %bitcast.55, bf16[2048,256]{1,0:T(8,128)(2,1)S(1)} %copy-done.3, f32[]{:T(128)} %constant.13.clone.1), kind=kCustom, calls=%fused_computation.18 | custom fusion | flops 1572864 | bytes 2097664 | tf_op jit(solution)/shard_map/scatter-add | solution.py:104
  596.0 2.5 multiply_add_fusion
  598.4 1.0 gather_fusion.6
  599.4 1.3 fusion.17
  601.2 206.7 %reduce-scatter.5.cloned.1.call-done = f32[8,256]{1,0:T(8,128)} async-done(((f32[256,256]{1,0:T(8,128)}), f32[8,256]{1,0:T(8,128)}) %reduce-scatter.5.cloned.1.call-update) | async-done | bytes 8208 | tf_op jit(solution)/shard_map/reduce_scatter | solution.py:93
  807.9 1.0 fusion.58
  808.9 82.9 %all-reduce.7 = bf16[512,256]{1,0:T(8,128)(2,1)S(1)} all-reduce(f32[512,256]{1,0:T(8,128)S(1)} %fusion.58), channel_id=1, replica_groups=mesh['rows'=8,'pts'=32] {'rows','pts'}, use_global_device_ids=true, to_apply=%region_16.17 | all-reduce | flops 131072 | bytes 786432 | tf_op jit(solution)/shard_map/psum | solution.py:96
  891.9 2.1 fusion.29
  894.0 99.8 %all-gather.5.cloned.1.call-done = bf16[2048,256]{1,0:T(8,128)(2,1)} async-done(((bf16[8,256]{1,0:T(8,128)(2,1)}), bf16[2048,256]{1,0:T(8,128)(2,1)}) %all-gather.5.cloned.1.call-update) | async-done | bytes 1048592 | tf_op jit(solution)/shard_map/all_gather | solution.py:98
  993.8 12.5 %scatter_custom_fusion.2 = f32[1024,256]{1,0:T(8,128)S(1)} fusion(f32[1024,256]{1,0:T(8,128)S(1)} %get-tuple-element.7, s32[2048]{0:T(1024)S(1)} %bitcast.52, bf16[2048,256]{1,0:T(8,128)(2,1)} %all-gather.5.cloned.1.call-done, f32[]{:T(128)} %constant.14.clone.1), kind=kCustom, calls=%fused_computation.20 | custom fusion | flops 1572864 | bytes 2097156 | tf_op jit(solution)/shard_map/scatter-add | solution.py:100
  1006.3 14.1 %scatter_custom_fusion.3 = f32[1024,256]{1,0:T(8,128)} fusion(f32[1024,256]{1,0:T(8,128)} %get-tuple-element.6, s32[2048]{0:T(1024)S(1)} %bitcast.53, bf16[2048,256]{1,0:T(8,128)(2,1)S(1)} %copy-done.4, f32[]{:T(128)} %constant.13.clone.1), kind=kCustom, calls=%fused_computation.21 | custom fusion | flops 1572864 | bytes 2097664 | tf_op jit(solution)/shard_map/scatter-add | solution.py:104
  (59 shorter events, 6.0 us)
Async XLA Ops:
  7.2 19.2 %copy-start = (bf16[1024,256]{1,0:T(8,128)(2,1)S(1)}, bf16[1024,256]{1,0:T(8,128)(2,1)}, u32[]{:S(2)}) copy-start(bf16[1024,256]{1,0:T(8,128)(2,1)} %param.8) | copy-start | bytes 1572868
  7.2 160.9 %all-reduce.5.cloned.1.call-start = ((), (), s32[]{:S(2)}) async-start(), calls=%async_computation.6 | async-start | bytes 786432 | tf_op jit(solution)/shard_map/psum | solution.py:78
  12.1 3.2 copy-start.1
  18.4 4.5 copy-start.5
  22.8 360.7 %reduce-scatter.3.cloned.1.call-start = ((), (), s32[]{:S(2)}) async-start(), calls=%async_computation.2 | async-start | bytes 270336 | tf_op jit(solution)/shard_map/reduce_scatter | solution.py:93
  169.0 3.0 copy-start.7
  171.2 398.3 %all-gather.3.cloned.1.call-start = ((), (), s32[]{:S(2)}) async-start(), calls=%async_computation.3 | async-start | bytes 1052672 | tf_op jit(solution)/shard_map/all_gather | solution.py:98
  383.5 84.0 %copy-start.10 = (f32[8,256]{1,0:T(8,128)S(1)}, f32[8,256]{1,0:T(8,128)}, u32[]{:S(2)}) copy-start(f32[8,256]{1,0:T(8,128)} %reduce-scatter.3.cloned.1.call-done) | copy-start | bytes 24580
  467.5 3.4 copy-start.9
  467.5 3.4 copy-start.8
  469.7 338.1 %reduce-scatter.5.cloned.1.call-start = ((), (), s32[]{:S(2)}) async-start(), calls=%async_computation.4 | async-start | bytes 270336 | tf_op jit(solution)/shard_map/reduce_scatter | solution.py:93
  569.5 12.7 %copy-start.3 = (bf16[2048,256]{1,0:T(8,128)(2,1)S(1)}, bf16[2048,256]{1,0:T(8,128)(2,1)}, u32[]{:S(2)}) copy-start(bf16[2048,256]{1,0:T(8,128)(2,1)} %all-gather.3.cloned.1.call-done) | copy-start | bytes 3145732
  599.4 1.5 copy-start.6
  600.7 393.1 %all-gather.5.cloned.1.call-start = ((), (), s32[]{:S(2)}) async-start(), calls=%async_computation.5 | async-start | bytes 1052672 | tf_op jit(solution)/shard_map/all_gather | solution.py:98
  807.9 84.0 %copy-start.11 = (f32[8,256]{1,0:T(8,128)S(1)}, f32[8,256]{1,0:T(8,128)}, u32[]{:S(2)}) copy-start(f32[8,256]{1,0:T(8,128)} %reduce-scatter.5.cloned.1.call-done) | copy-start | bytes 24580
  993.8 12.5 %copy-start.4 = (bf16[2048,256]{1,0:T(8,128)(2,1)S(1)}, bf16[2048,256]{1,0:T(8,128)(2,1)}, u32[]{:S(2)}) copy-start(bf16[2048,256]{1,0:T(8,128)(2,1)} %all-gather.5.cloned.1.call-done) | copy-start | bytes 3145732
  1006.3 14.2 %copy-start.2 = (f32[1024,256]{1,0:T(8,128)}, f32[1024,256]{1,0:T(8,128)S(1)}, u32[]{:S(2)}) copy-start(f32[1024,256]{1,0:T(8,128)S(1)} %scatter_custom_fusion.2) | copy-start | bytes 3145732
Sparse Core Ops, SparseCore 0:
  22.9 145.1 all-reduce.4
  172.9 210.5 reduce-scatter.2
  469.8 99.5 all-gather.2
  600.8 206.9 reduce-scatter.4
  894.1 99.5 all-gather.4
where the time goes:
time: 1030 us
  waiting for transfers between devices  756 us (73%)
  blocking collectives  166 us (16%)
  other arithmetic  64.6 us (6%)
  local copies, waits for them, and re-layouts  15.8 us (2%)
  between operations  14.1 us (1%)
  matrix products  10.7 us (1%)
    reduce_scatter x2, waiting for transfers between devices, shards(): lax.psum_scatter(partial_value, 'pts', scatter_dimension=0, tiled=True)  417 us
    all_gather x2, waiting for transfers between devices, shards(): steps = lax.all_gather(step_bf, ('rows', 'pts'), axis=0, tiled=True)  198 us
    psum x2, blocking collectives, shards(): proj = lax.psum(project_rows(factor, resid), ('rows', 'pts'))  166 us
    psum x1, waiting for transfers between devices, shards(): lax.psum(row_terms, 'pts').astype(jnp.float32)  140 us
    scatter-add x2, other arithmetic, shards(): momentum_now = (beta_keep * momentum_now + (1.0 - beta_keep) * mixed).at[...  27.9 us
    scatter-add x2, other arithmetic, shards(): current = mixed.at[whole_slots].add(-step_size * change, mode='drop')  25.2 us
  transfers between devices with their start and end apart: 5, of which 5 were waited for; matrix products, arithmetic and copies ran while one was open for 1% of the time, Pallas kernels for 0%

commit v1 on v0

--- a/solution.py
+++ b/solution.py
@@ -93,7 +93,7 @@
         resid = lax.psum_scatter(partial_value, "pts", scatter_dimension=0, tiled=True)
         share_feats = lax.dynamic_slice_in_dim(block_feats, pts_id * per_device, per_device)
         factor = kernel_tile(share_feats, pivot_feats)
-        proj = lax.psum(project_rows(factor, resid), ("rows", "pts"))
+        proj = lax.psum(lax.psum(project_rows(factor, resid), "pts"), "rows")
         step_bf = finish_step(resid, factor, proj, nystrom_core[update])
         steps = lax.all_gather(step_bf, ("rows", "pts"), axis=0, tiled=True)
         change = steps.astype(jnp.float32)

time: 1030 us -> 1220 us (1.18)
  waiting for transfers between devices: 756 us -> 1050 us
  blocking collectives: 166 us -> 62.6 us
    psum x0 -> x2, waiting for transfers between devices: none -> 297 us  [shards(): proj = lax.psum(lax.psum(project_rows(factor, resid), 'pts'), 'rows')]
    psum x2, blocking collectives: 166 us -> 62.6 us  [shards(): proj = lax.psum(lax.psum(project_rows(factor, resid), 'pts'), 'rows')]
  transfers between devices with their start and end apart: 5 -> 7, of which waited for: 5 -> 7; matrix products, arithmetic and copies ran while one was open for 1% -> 1% of each run, Pallas kernels for 0% -> 0%
where the time goes in v1:
time: 1220 us
  waiting for transfers between devices  1050 us (86%)
  other arithmetic  64.3 us (5%)
  blocking collectives  62.6 us (5%)
  local copies, waits for them, and re-layouts  15.8 us (1%)
  between operations  14.5 us (1%)
  matrix products  12.3 us (1%)
    reduce_scatter x2, waiting for transfers between devices, shards(): lax.psum_scatter(partial_value, 'pts', scatter_dimension=0, tiled=True)  417 us
    psum x2, waiting for transfers between devices, shards(): proj = lax.psum(lax.psum(project_rows(factor, resid), 'pts'), 'rows')  297 us
    all_gather x2, waiting for transfers between devices, shards(): steps = lax.all_gather(step_bf, ('rows', 'pts'), axis=0, tiled=True)  199 us
    psum x1, waiting for transfers between devices, shards(): lax.psum(row_terms, 'pts').astype(jnp.float32)  140 us
    psum x2, blocking collectives, shards(): proj = lax.psum(lax.psum(project_rows(factor, resid), 'pts'), 'rows')  62.6 us
    scatter-add x2, other arithmetic, shards(): momentum_now = (beta_keep * momentum_now + (1.0 - beta_keep) * mixed).at[...  27.9 us
    scatter-add x2, other arithmetic, shards(): current = mixed.at[whole_slots].add(-step_size * change, mode='drop')  25 us
  transfers between devices with their start and end apart: 7, of which 7 were waited for; matrix products, arithmetic and copies ran while one was open for 1% of the time, Pallas kernels for 0%

profile of v1, /device:TPU:1, one launch (start us, length us, event | category | flops | bytes accessed | tf_op | source)
XLA Modules:
  0.0 1223.6 jit_solution(15814607811181337584)
XLA Ops:
  8.9 3.1 gather_fusion.8
  12.1 3.1 gather_fusion.3
  15.3 0.9 gather_fusion
  16.2 1.3 gather_fusion.4
  17.5 0.9 gather_fusion.5
  18.4 1.3 gather_fusion.9
  22.9 2.5 multiply_add_fusion.2
  25.3 1.0 gather_fusion.1
  26.3 1.2 gather_fusion.2
  27.7 140.4 %all-reduce.11.cloned.1.call-done = (bf16[256,128]{1,0:T(8,128)(2,1)}, bf16[512,128]{1,0:T(8,128)(2,1)}, bf16[256,128]{1,0:T(8,128)(2,1)}, bf16[512,128]{1,0:T(8,128)(2,1)}) async-done(((bf16[256,128]{1,0:T(8,128)(2,1)}, bf16[512,128]{1,0:T(8,128)(2,1)}, bf16[256,128]{1,0:T(8,128)(2,1)}, bf16[512,128]{1,0:T(8,128)(2,1)}), (bf16[256,128]{1,0:T(8,128)(2,1)}, bf16[512,128]{1,0:T(8,128)(2,1)}, ...) | async-done | bytes 393232 | tf_op jit(solution)/shard_map/psum | solution.py:78
  168.1 0.9 multiply_reduce_fusion.4
  169.0 2.1 fusion.16
  173.0 210.5 %reduce-scatter.3.cloned.1.call-done = f32[8,256]{1,0:T(8,128)} async-done(((f32[256,256]{1,0:T(8,128)}), f32[8,256]{1,0:T(8,128)}) %reduce-scatter.3.cloned.1.call-update) | async-done | bytes 8208 | tf_op jit(solution)/shard_map/reduce_scatter | solution.py:93
  383.5 1.8 fusion.60
  385.4 148.8 %all-reduce.7.cloned.1.call-done = f32[512,256]{1,0:T(8,128)} async-done(((f32[512,256]{1,0:T(8,128)}), f32[512,256]{1,0:T(8,128)}) %all-reduce.7.cloned.1.call-update) | async-done | bytes 524304 | tf_op jit(solution)/shard_map/psum | solution.py:96
  534.2 31.3 %all-reduce.12 = bf16[512,256]{1,0:T(8,128)(2,1)S(1)} all-reduce(f32[512,256]{1,0:T(8,128)} %all-reduce.7.cloned.1.call-done), channel_id=1, replica_groups=mesh['rows'=8,'pts'=32] {'rows'}, use_global_device_ids=true, to_apply=%region_8.9 | all-reduce | flops 131072 | bytes 786432 | tf_op jit(solution)/shard_map/psum | solution.py:96
  565.5 2.1 fusion.28
  567.7 1.2 gather_fusion.7
  569.1 98.7 %all-gather.3.cloned.1.call-done = bf16[2048,256]{1,0:T(8,128)(2,1)} async-done(((bf16[8,256]{1,0:T(8,128)(2,1)}), bf16[2048,256]{1,0:T(8,128)(2,1)}) %all-gather.3.cloned.1.call-update) | async-done | bytes 1048592 | tf_op jit(solution)/shard_map/all_gather | solution.py:98
  667.8 12.5 %scatter_custom_fusion.1 = f32[1024,256]{1,0:T(8,128)S(1)} fusion(f32[1024,256]{1,0:T(8,128)S(1)} %get-tuple-element.9, s32[2048]{0:T(1024)S(1)} %bitcast.54, bf16[2048,256]{1,0:T(8,128)(2,1)} %all-gather.3.cloned.1.call-done, f32[]{:T(128)} %constant.14.clone.1), kind=kCustom, calls=%fused_computation.19 | custom fusion | flops 1572864 | bytes 2097156 | tf_op jit(solution)/shard_map/scatter-add | solution.py:100
  680.3 13.8 %scatter_custom_fusion = f32[1024,256]{1,0:T(8,128)} fusion(f32[1024,256]{1,0:T(8,128)} %get-tuple-element.8, s32[2048]{0:T(1024)S(1)} %bitcast.55, bf16[2048,256]{1,0:T(8,128)(2,1)S(1)} %copy-done.3, f32[]{:T(128)} %constant.13.clone.1), kind=kCustom, calls=%fused_computation.18 | custom fusion | flops 1572864 | bytes 2097664 | tf_op jit(solution)/shard_map/scatter-add | solution.py:104
  694.1 2.5 multiply_add_fusion
  696.6 1.0 gather_fusion.6
  697.5 1.3 fusion.17
  699.3 206.7 %reduce-scatter.5.cloned.1.call-done = f32[8,256]{1,0:T(8,128)} async-done(((f32[256,256]{1,0:T(8,128)}), f32[8,256]{1,0:T(8,128)}) %reduce-scatter.5.cloned.1.call-update) | async-done | bytes 8208 | tf_op jit(solution)/shard_map/reduce_scatter | solution.py:93
  906.0 1.8 fusion.58
  907.9 148.6 %all-reduce.9.cloned.1.call-done = f32[512,256]{1,0:T(8,128)} async-done(((f32[512,256]{1,0:T(8,128)}), f32[512,256]{1,0:T(8,128)}) %all-reduce.9.cloned.1.call-update) | async-done | bytes 524304 | tf_op jit(solution)/shard_map/psum | solution.py:96
  1056.5 31.3 %all-reduce.13 = bf16[512,256]{1,0:T(8,128)(2,1)S(1)} all-reduce(f32[512,256]{1,0:T(8,128)} %all-reduce.9.cloned.1.call-done), channel_id=1, replica_groups=mesh['rows'=8,'pts'=32] {'rows'}, use_global_device_ids=true, to_apply=%region_18.19 | all-reduce | flops 131072 | bytes 786432 | tf_op jit(solution)/shard_map/psum | solution.py:96
  1087.8 2.1 fusion.29
  1089.9 100.1 %all-gather.5.cloned.1.call-done = bf16[2048,256]{1,0:T(8,128)(2,1)} async-done(((bf16[8,256]{1,0:T(8,128)(2,1)}), bf16[2048,256]{1,0:T(8,128)(2,1)}) %all-gather.5.cloned.1.call-update) | async-done | bytes 1048592 | tf_op jit(solution)/shard_map/all_gather | solution.py:98
  1190.0 12.5 %scatter_custom_fusion.2 = f32[1024,256]{1,0:T(8,128)S(1)} fusion(f32[1024,256]{1,0:T(8,128)S(1)} %get-tuple-element.7, s32[2048]{0:T(1024)S(1)} %bitcast.52, bf16[2048,256]{1,0:T(8,128)(2,1)} %all-gather.5.cloned.1.call-done, f32[]{:T(128)} %constant.14.clone.1), kind=kCustom, calls=%fused_computation.20 | custom fusion | flops 1572864 | bytes 2097156 | tf_op jit(solution)/shard_map/scatter-add | solution.py:100
  1202.6 14.1 %scatter_custom_fusion.3 = f32[1024,256]{1,0:T(8,128)} fusion(f32[1024,256]{1,0:T(8,128)} %get-tuple-element.6, s32[2048]{0:T(1024)S(1)} %bitcast.53, bf16[2048,256]{1,0:T(8,128)(2,1)S(1)} %copy-done.4, f32[]{:T(128)} %constant.13.clone.1), kind=kCustom, calls=%fused_computation.21 | custom fusion | flops 1572864 | bytes 2097664 | tf_op jit(solution)/shard_map/scatter-add | solution.py:104
  (65 shorter events, 7.7 us)
Async XLA Ops:
  7.2 19.1 %copy-start = (bf16[1024,256]{1,0:T(8,128)(2,1)S(1)}, bf16[1024,256]{1,0:T(8,128)(2,1)}, u32[]{:S(2)}) copy-start(bf16[1024,256]{1,0:T(8,128)(2,1)} %param.8) | copy-start | bytes 1572868
  7.2 160.9 %all-reduce.11.cloned.1.call-start = ((), (), s32[]{:S(2)}) async-start(), calls=%async_computation.8 | async-start | bytes 786432 | tf_op jit(solution)/shard_map/psum | solution.py:78
  12.1 3.2 copy-start.1
  18.4 4.5 copy-start.5
  22.8 360.7 %reduce-scatter.3.cloned.1.call-start = ((), (), s32[]{:S(2)}) async-start(), calls=%async_computation.2 | async-start | bytes 270336 | tf_op jit(solution)/shard_map/reduce_scatter | solution.py:93
  169.0 3.0 copy-start.7
  171.2 363.0 %all-reduce.7.cloned.1.call-start = ((), (), s32[]{:S(2)}) async-start(), calls=%async_computation.3 | async-start | bytes 1048576 | tf_op jit(solution)/shard_map/psum | solution.py:96
  383.5 182.0 %copy-start.10 = (f32[8,256]{1,0:T(8,128)S(1)}, f32[8,256]{1,0:T(8,128)}, u32[]{:S(2)}) copy-start(f32[8,256]{1,0:T(8,128)} %reduce-scatter.3.cloned.1.call-done) | copy-start | bytes 24580
  385.4 282.4 %all-gather.3.cloned.1.call-start = ((), (), s32[]{:S(2)}) async-start(), calls=%async_computation.4 | async-start | bytes 1052672 | tf_op jit(solution)/shard_map/all_gather | solution.py:98
  565.5 3.4 copy-start.9
  565.5 3.4 copy-start.8
  567.7 338.3 %reduce-scatter.5.cloned.1.call-start = ((), (), s32[]{:S(2)}) async-start(), calls=%async_computation.5 | async-start | bytes 270336 | tf_op jit(solution)/shard_map/reduce_scatter | solution.py:93
  667.8 12.5 %copy-start.3 = (bf16[2048,256]{1,0:T(8,128)(2,1)S(1)}, bf16[2048,256]{1,0:T(8,128)(2,1)}, u32[]{:S(2)}) copy-start(bf16[2048,256]{1,0:T(8,128)(2,1)} %all-gather.3.cloned.1.call-done) | copy-start | bytes 3145732
  697.5 1.5 copy-start.6
  698.8 357.7 %all-reduce.9.cloned.1.call-start = ((), (), s32[]{:S(2)}) async-start(), calls=%async_computation.6 | async-start | bytes 1048576 | tf_op jit(solution)/shard_map/psum | solution.py:96
  906.0 181.8 %copy-start.11 = (f32[8,256]{1,0:T(8,128)S(1)}, f32[8,256]{1,0:T(8,128)}, u32[]{:S(2)}) copy-start(f32[8,256]{1,0:T(8,128)} %reduce-scatter.5.cloned.1.call-done) | copy-start | bytes 24580
  907.8 282.2 %all-gather.5.cloned.1.call-start = ((), (), s32[]{:S(2)}) async-start(), calls=%async_computation.7 | async-start | bytes 1052672 | tf_op jit(solution)/shard_map/all_gather | solution.py:98
  1190.0 12.5 %copy-start.4 = (bf16[2048,256]{1,0:T(8,128)(2,1)S(1)}, bf16[2048,256]{1,0:T(8,128)(2,1)}, u32[]{:S(2)}) copy-start(bf16[2048,256]{1,0:T(8,128)(2,1)} %all-gather.5.cloned.1.call-done) | copy-start | bytes 3145732
  1202.6 14.2 %copy-start.2 = (f32[1024,256]{1,0:T(8,128)}, f32[1024,256]{1,0:T(8,128)S(1)}, u32[]{:S(2)}) copy-start(f32[1024,256]{1,0:T(8,128)S(1)} %scatter_custom_fusion.2) | copy-start | bytes 3145732
Sparse Core Ops, SparseCore 0:
  22.9 145.1 all-reduce.10
  172.9 210.5 reduce-scatter.2
  387.5 146.6 all-reduce.6
  567.8 99.9 all-gather.2
  698.9 206.9 reduce-scatter.4
  909.8 146.6 all-reduce.8
  1090.1 99.9 all-gather.4
